TPU v7x, 32 devices: a whole 2x2x4 slice. The times are simulated.
32 devices in a mesh: groups: 2 (over y), row: 4 (over z), col: 2 (over x), rep: 2 (over core).
Axes of the slice: x: 2, y: 2, z: 4, core: 2. Of those that a mesh axis runs over, the one named last changes fastest.
Arguments:
- kernel: float32 [32768, 16384], P(('groups', 'row'), ('col', 'rep')), parts along dimension 0, may hold values from 0 to 2, as said below
- source: float32 [64, 16384], P('groups', 'row'), parts along dimension 0, may hold values from 0.5 to 2, as said below
- target: float32 [64, 16384], P('groups', ('col', 'rep')), parts along dimension 0, may hold values from 0.5 to 2, as said below
Outputs:
- left_scale: float32 [64, 16384], P('groups', 'row'), parts along dimension 0
- right_scale: float32 [64, 16384], P('groups', ('col', 'rep')), parts along dimension 0
- errors: float32 [6, 32], P('groups'), parts along dimension 0
There are 2 independent parts, one for each index of `groups`. A program takes and returns all parts, laid end to end along the dimension named above; each array names one. Nothing has to cross between parts.
Inputs may be any that keep to these rules, and one draw needn't show every extreme that they name: `kernel`: every entry is positive. `source`: every entry is positive. `target`: every entry is positive.
All inputs are finite; a program needn't handle non-finite values.
Results may differ from a plain program's by a relative error of at most 0.0001.
Values sent between devices are 32-bit elements; how exact they have to be, the bound alone decides.
A program may use at most 128 MiB of HBM per device.

v0:
```python
import jax
import jax.numpy as jnp
from jax import lax
from jax.sharding import PartitionSpec as P

N = 16384
ITERS = 3


def local(kernel, source, target):
    columns = kernel.shape[1]
    right_scale = jnp.ones(target.shape, jnp.float32)
    left_scale = source
    share = columns // lax.axis_size("row")
    offset = lax.axis_index("row") * share
    errors = []
    for step in range(ITERS):
        partial_value = lax.dot_general(
            right_scale, kernel, (((1,), (1,)), ((), ())), precision=lax.Precision.HIGHEST
        )
        left_scale = source / lax.psum(partial_value, ("col", "rep"))
        back = jnp.dot(left_scale, kernel, precision=lax.Precision.HIGHEST)
        old_piece = lax.dynamic_slice_in_dim(right_scale, offset, share, 1)
        target_piece = lax.dynamic_slice_in_dim(target, offset, share, 1)
        total_piece = lax.psum_scatter(back, "row", scatter_dimension=1, tiled=True)
        right_scale = lax.all_gather(target_piece / total_piece, "row", axis=1, tiled=True)
        term = jnp.sum(jnp.abs(old_piece * total_piece - target_piece), axis=1) / N
        errors.append(lax.psum(term, ("row", "col", "rep")))
    stacked = jnp.stack(errors)
    return (left_scale, right_scale, stacked)


def solution(mesh):
    return jax.shard_map(
        local,
        mesh=mesh,
        in_specs=(
            P(("groups", "row"), ("col", "rep")),
            P("groups", "row"),
            P("groups", ("col", "rep")),
        ),
        out_specs=(P("groups", "row"), P("groups", ("col", "rep")), P("groups", None)),
        check_vma=False,
    )
```

profile of v0, /device:TPU:0, one launch (start us, length us, event | category | flops | bytes accessed | tf_op | source)
XLA Modules:
  0.0 597.1 jit_solution(12538912805392526422)
XLA Ops:
  7.2 0.0 all-reduce.5.cloned.1.call-start
  7.2 66.4 %fusion.4 = f32[32,4096]{1,0:T(8,128)} fusion(f32[4096,4096]{1,0:T(8,128)} %param.3), kind=kOutput, calls=%fused_computation.4 | convolution fusion | flops 6442450944 | bytes 67633152 | tf_op jit(solution)/shard_map/dot_general | solution.py:18
  73.7 0.0 all-reduce.5.cloned.1.call-update
  73.7 0.3 reduce-scatter.4.cloned.1.call-start
  74.0 36.0 %all-reduce.5.cloned.1.call-done = f32[32,4096]{1,0:T(8,128)} async-done(((f32[32,4096]{1,0:T(8,128)}), f32[32,4096]{1,0:T(8,128)}) %all-reduce.5.cloned.1.call-update) | async-done | bytes 524304 | tf_op jit(solution)/shard_map/psum | solution.py:21
  110.0 44.8 %fusion.2 = f32[32,4096]{1,0:T(8,128)} fusion(f32[4096,4096]{1,0:T(8,128)} %param.3, f32[32,4096]{1,0:T(8,128)S(1)} %copy-done, f32[32,4096]{1,0:T(8,128)} %all-reduce.5.cloned.1.call-done), kind=kOutput, calls=%fused_computation.2 | convolution fusion | flops 6442582016 | bytes 68681728 | tf_op jit(solution)/shard_map/dot_general | solution.py:22
  154.8 0.0 reduce-scatter.4.cloned.1.call-update
  154.9 0.0 all-reduce.7.cloned.1.call-start
  154.9 22.1 %reduce-scatter.4.cloned.1.call-done = f32[32,1024]{1,0:T(8,128)} async-done(((f32[32,4096]{1,0:T(8,128)}), f32[32,1024]{1,0:T(8,128)}) %reduce-scatter.4.cloned.1.call-update) | async-done | bytes 131088 | tf_op jit(solution)/shard_map/reduce_scatter | solution.py:25
  177.0 0.9 dynamic-slice_divide_fusion.2
  177.9 15.7 %all_gather.9 = f32[32,4096]{1,0:T(8,128)S(1)} all-gather(f32[32,1024]{1,0:T(8,128)S(1)} %dynamic-slice_divide_fusion.2), channel_id=1, replica_groups=mesh['groups'=2,'row'=4,'col'=2,'rep'=2] {'row'}, dimensions={1}, use_global_device_ids=true | all-gather | bytes 655360 | tf_op jit(solution)/shard_map/all_gather | solution.py:26
  193.7 66.5 %fusion.7 = f32[32,4096]{1,0:T(8,128)} fusion(f32[32,4096]{1,0:T(8,128)S(1)} %all_gather.9, f32[4096,4096]{1,0:T(8,128)} %param.3), kind=kOutput, calls=%fused_computation.17 | convolution fusion | flops 6442450944 | bytes 68157440 | tf_op jit(solution)/shard_map/dot_general | solution.py:18
  260.2 0.0 all-reduce.7.cloned.1.call-update
  260.2 0.2 reduce-scatter.6.cloned.1.call-start
  260.4 31.8 %all-reduce.7.cloned.1.call-done = f32[32,4096]{1,0:T(8,128)} async-done(((f32[32,4096]{1,0:T(8,128)}), f32[32,4096]{1,0:T(8,128)}) %all-reduce.7.cloned.1.call-update) | async-done | bytes 524304 | tf_op jit(solution)/shard_map/psum | solution.py:21
  292.2 44.8 %fusion = f32[32,4096]{1,0:T(8,128)} fusion(f32[4096,4096]{1,0:T(8,128)} %param.3, f32[32,4096]{1,0:T(8,128)S(1)} %copy-done, f32[32,4096]{1,0:T(8,128)} %all-reduce.7.cloned.1.call-done), kind=kOutput, calls=%fused_computation | convolution fusion | flops 6442582016 | bytes 68681728 | tf_op jit(solution)/shard_map/dot_general | solution.py:22
  337.0 0.0 all-reduce.9.cloned.1.call-start
  337.1 22.0 %reduce-scatter.6.cloned.1.call-done = f32[32,1024]{1,0:T(8,128)} async-done(((f32[32,4096]{1,0:T(8,128)}), f32[32,1024]{1,0:T(8,128)}) %reduce-scatter.6.cloned.1.call-update) | async-done | bytes 131088 | tf_op jit(solution)/shard_map/reduce_scatter | solution.py:25
  359.1 0.9 dynamic-slice_divide_fusion.1
  360.0 15.7 %all_gather.10 = f32[32,4096]{1,0:T(8,128)S(1)} all-gather(f32[32,1024]{1,0:T(8,128)S(1)} %dynamic-slice_divide_fusion.1), channel_id=1, replica_groups=mesh['groups'=2,'row'=4,'col'=2,'rep'=2] {'row'}, dimensions={1}, use_global_device_ids=true | all-gather | bytes 655360 | tf_op jit(solution)/shard_map/all_gather | solution.py:26
  375.7 66.5 %fusion.8 = f32[32,4096]{1,0:T(8,128)} fusion(f32[32,4096]{1,0:T(8,128)S(1)} %all_gather.10, f32[4096,4096]{1,0:T(8,128)} %param.3), kind=kOutput, calls=%fused_computation.18 | convolution fusion | flops 6442450944 | bytes 68157440 | tf_op jit(solution)/shard_map/dot_general | solution.py:18
  442.2 0.0 all-reduce.9.cloned.1.call-update
  442.2 0.3 reduce-scatter.8.cloned.1.call-start
  442.5 31.6 %all-reduce.9.cloned.1.call-done = f32[32,4096]{1,0:T(8,128)} async-done(((f32[32,4096]{1,0:T(8,128)}), f32[32,4096]{1,0:T(8,128)}) %all-reduce.9.cloned.1.call-update) | async-done | bytes 524304 | tf_op jit(solution)/shard_map/psum | solution.py:21
  474.2 1.1 div.31
  475.3 45.0 %fusion.9 = f32[32,4096]{1,0:T(8,128)} fusion(f32[32,4096]{1,0:T(8,128)S(1)} %div.31, f32[4096,4096]{1,0:T(8,128)} %param.3), kind=kOutput, calls=%fused_computation.19 | convolution fusion | flops 6442450944 | bytes 68157440 | tf_op jit(solution)/shard_map/dot_general | solution.py:22
  520.4 22.1 %reduce-scatter.8.cloned.1.call-done = f32[32,1024]{1,0:T(8,128)} async-done(((f32[32,4096]{1,0:T(8,128)}), f32[32,1024]{1,0:T(8,128)}) %reduce-scatter.8.cloned.1.call-update) | async-done | bytes 131088 | tf_op jit(solution)/shard_map/reduce_scatter | solution.py:25
  542.5 1.1 abs_reduce_fusion.2
  543.6 15.3 %all_gather.11 = f32[32,4096]{1,0:T(8,128)S(1)} all-gather(f32[32,1024]{1,0:T(8,128)S(1)} %get-tuple-element.9), channel_id=1, replica_groups=mesh['groups'=2,'row'=4,'col'=2,'rep'=2] {'row'}, dimensions={1}, use_global_device_ids=true | all-gather | bytes 655360 | tf_op jit(solution)/shard_map/all_gather | solution.py:26
  558.9 29.5 %all-reduce = (f32[1,32]{1,0:T(1,128)S(1)}, f32[1,32]{1,0:T(1,128)S(1)}, f32[1,32]{1,0:T(1,128)S(1)}) all-reduce(f32[1,32]{1,0:T(1,128)S(1)} %get-tuple-element.10, f32[1,32]{1,0:T(1,128)S(1)} %get-tuple-element.11, f32[1,32]{1,0:T(1,128)S(1)} %multiply_bitcast_fusion.2), channel_id=1, replica_groups=mesh['groups'=2,'row'=4,'col'=2,'rep'=2] {'row','col','rep'}, use_global_device_ids=true, to_apply=%region_11.0 | all-reduce | flops 96 | bytes 768 | tf_op jit(solution)/shard_map/psum | solution.py:28
  588.4 0.6 pad_maximum_fusion
  589.0 0.8 copy.10
  (14 shorter events, 0.1 us)
Async XLA Ops:
  7.2 102.8 %copy-start = (f32[32,4096]{1,0:T(8,128)S(1)}, f32[32,4096]{1,0:T(8,128)}, u32[]{:S(2)}) copy-start(f32[32,4096]{1,0:T(8,128)} %param.4) | copy-start | bytes 1572868
  7.2 102.8 %all-reduce.5.cloned.1.call-start = ((), (), s32[]{:S(2)}) async-start(), calls=%async_computation.3 | async-start | bytes 1048576 | tf_op jit(solution)/shard_map/psum | solution.py:21
  73.7 103.3 %copy-start.4 = (f32[32,4096]{1,0:T(8,128)S(1)}, f32[32,4096]{1,0:T(8,128)}, u32[]{:S(2)}) copy-start(f32[32,4096]{1,0:T(8,128)} %param.5) | copy-start | bytes 1572868
  73.7 103.3 %reduce-scatter.4.cloned.1.call-start = ((), (), s32[]{:S(2)}) async-start(), calls=%async_computation.4 | async-start | bytes 655360 | tf_op jit(solution)/shard_map/reduce_scatter | solution.py:25
  154.9 137.3 %all-reduce.7.cloned.1.call-start = ((), (), s32[]{:S(2)}) async-start(), calls=%async_computation.5 | async-start | bytes 1048576 | tf_op jit(solution)/shard_map/psum | solution.py:21
  260.2 98.9 %reduce-scatter.6.cloned.1.call-start = ((), (), s32[]{:S(2)}) async-start(), calls=%async_computation.6 | async-start | bytes 655360 | tf_op jit(solution)/shard_map/reduce_scatter | solution.py:25
  337.0 137.1 %all-reduce.9.cloned.1.call-start = ((), (), s32[]{:S(2)}) async-start(), calls=%async_computation.7 | async-start | bytes 1048576 | tf_op jit(solution)/shard_map/psum | solution.py:21
  442.2 100.3 %copy-start.2 = (f32[32,1024]{1,0:T(8,128)S(1)}, f32[32,1024]{1,0:T(8,128)}, u32[]{:S(2)}) copy-start(f32[32,1024]{1,0:T(8,128)} %reduce-scatter.4.cloned.1.call-done) | copy-start | bytes 393220
  442.2 100.3 %copy-start.3 = (f32[32,1024]{1,0:T(8,128)S(1)}, f32[32,1024]{1,0:T(8,128)}, u32[]{:S(2)}) copy-start(f32[32,1024]{1,0:T(8,128)} %reduce-scatter.6.cloned.1.call-done) | copy-start | bytes 393220
  442.2 100.2 %reduce-scatter.8.cloned.1.call-start = ((), (), s32[]{:S(2)}) async-start(), calls=%async_computation.8 | async-start | bytes 655360 | tf_op jit(solution)/shard_map/reduce_scatter | solution.py:25
  475.3 114.5 %copy-start.1 = (f32[32,4096]{1,0:T(8,128)}, f32[32,4096]{1,0:T(8,128)S(1)}, u32[]{:S(2)}) copy-start(f32[32,4096]{1,0:T(8,128)S(1)} %div.31) | copy-start | bytes 1572868
Sparse Core Ops, SparseCore 0:
  73.8 36.1 all-reduce.4
  155.0 21.9 reduce-scatter.3
  260.3 31.8 all-reduce.6
  337.1 21.9 reduce-scatter.5
  442.4 31.7 all-reduce.8
  520.5 21.9 reduce-scatter.7
where the time goes:
time: 606 us; the launch traced here: 597 us
  matrix products  334 us (55%)
  waiting for transfers between devices  166 us (27%)
  blocking collectives  76.2 us (13%)
  between operations  14.6 us (2%)
    dot_general x3, matrix products, local(): lax.dot_general(right_scale, kernel, (((1,), (1,)), ((), ())), precision=...  199 us
    dot_general x3, matrix products, local(): back = jnp.dot(left_scale, kernel, precision=lax.Precision.HIGHEST)  135 us
    psum x3, waiting for transfers between devices, local(): left_scale = source / lax.psum(partial_value, ('col', 'rep'))  99.4 us
    reduce_scatter x3, waiting for transfers between devices, local(): total_piece = lax.psum_scatter(back, 'row', scatter_dimension=1, tiled=True)  66.2 us
    all_gather x3, blocking collectives, local(): lax.all_gather(target_piece / total_piece, 'row', axis=1, tiled=True)  46.8 us
    psum x1, blocking collectives, local(): errors.append(lax.psum(term, ('row', 'col', 'rep')))  29.5 us
  transfers between devices with their start and end apart: 6, of which 6 were waited for; matrix products, arithmetic and copies ran while one was open for 0% of the time, Pallas kernels for 0%

commit v1 on v0

--- a/solution.py
+++ b/solution.py
@@ -18,7 +18,7 @@
         partial_value = lax.dot_general(
             right_scale, kernel, (((1,), (1,)), ((), ())), precision=lax.Precision.HIGHEST
         )
-        left_scale = source / lax.psum(partial_value, ("col", "rep"))
+        left_scale = source / lax.psum(lax.psum(partial_value, "col"), "rep")
         back = jnp.dot(left_scale, kernel, precision=lax.Precision.HIGHEST)
         old_piece = lax.dynamic_slice_in_dim(right_scale, offset, share, 1)
         target_piece = lax.dynamic_slice_in_dim(target, offset, share, 1)

time: 606 us -> 657 us (1.084)
  waiting for transfers between devices: 166 us -> 217 us
    psum x3 -> x6, waiting for transfers between devices: 99.4 us -> 148 us  [local(): left_scale = source / lax.psum(lax.psum(partial_value, 'col'), 'rep')]
  transfers between devices with their start and end apart: 6 -> 9, of which waited for: 6 -> 9; matrix products, arithmetic and copies ran while one was open for 0% -> 0% of each run, Pallas kernels for 0% -> 0%
where the time goes in v1:
time: 657 us; the launch traced here: 649 us
  matrix products  334 us (51%)
  waiting for transfers between devices  217 us (33%)
  blocking collectives  76.4 us (12%)
  between operations  14.3 us (2%)
    dot_general x3, matrix products, local(): lax.dot_general(right_scale, kernel, (((1,), (1,)), ((), ())), precision=...  199 us
    psum x6, waiting for transfers between devices, local(): left_scale = source / lax.psum(lax.psum(partial_value, 'col'), 'rep')  148 us
    dot_general x3, matrix products, local(): back = jnp.dot(left_scale, kernel, precision=lax.Precision.HIGHEST)  135 us
    reduce_scatter x3, waiting for transfers between devices, local(): total_piece = lax.psum_scatter(back, 'row', scatter_dimension=1, tiled=True)  69.5 us
    all_gather x3, blocking collectives, local(): lax.all_gather(target_piece / total_piece, 'row', axis=1, tiled=True)  46.9 us
    psum x1, blocking collectives, local(): errors.append(lax.psum(term, ('row', 'col', 'rep')))  29.5 us
  transfers between devices with their start and end apart: 9, of which 9 were waited for; matrix products, arithmetic and copies ran while one was open for 0% of the time, Pallas kernels for 0%

profile of v1, /device:TPU:0, one launch (start us, length us, event | category | flops | bytes accessed | tf_op | source)
XLA Modules:
  0.0 648.8 jit_solution(10131668350359479121)
XLA Ops:
  7.2 66.4 %fusion.4 = f32[32,4096]{1,0:T(8,128)} fusion(f32[4096,4096]{1,0:T(8,128)} %param.3), kind=kOutput, calls=%fused_computation.4 | convolution fusion | flops 6442450944 | bytes 67633152 | tf_op jit(solution)/shard_map/dot_general | solution.py:18
  73.7 31.5 %all-reduce.8.cloned.1.call-done = f32[32,4096]{1,0:T(8,128)} async-done(((f32[32,4096]{1,0:T(8,128)}), f32[32,4096]{1,0:T(8,128)}) %all-reduce.8.cloned.1.call-update) | async-done | bytes 524304 | tf_op jit(solution)/shard_map/psum | solution.py:21
  105.3 0.3 reduce-scatter.4.cloned.1.call-start
  105.5 20.7 %all-reduce.10.cloned.1.call-done = f32[32,4096]{1,0:T(8,128)} async-done(((f32[32,4096]{1,0:T(8,128)}), f32[32,4096]{1,0:T(8,128)}) %all-reduce.10.cloned.1.call-update) | async-done | bytes 524304 | tf_op jit(solution)/shard_map/psum | solution.py:21
  126.2 44.8 %fusion.2 = f32[32,4096]{1,0:T(8,128)} fusion(f32[4096,4096]{1,0:T(8,128)} %param.3, f32[32,4096]{1,0:T(8,128)S(1)} %copy-done, f32[32,4096]{1,0:T(8,128)} %all-reduce.10.cloned.1.call-done), kind=kOutput, calls=%fused_computation.2 | convolution fusion | flops 6442582016 | bytes 68681728 | tf_op jit(solution)/shard_map/dot_general | solution.py:22
  171.1 0.0 all-reduce.12.cloned.1.call-start
  171.1 23.2 %reduce-scatter.4.cloned.1.call-done = f32[32,1024]{1,0:T(8,128)} async-done(((f32[32,4096]{1,0:T(8,128)}), f32[32,1024]{1,0:T(8,128)}) %reduce-scatter.4.cloned.1.call-update) | async-done | bytes 131088 | tf_op jit(solution)/shard_map/reduce_scatter | solution.py:25
  194.3 0.9 dynamic-slice_divide_fusion.2
  195.2 15.9 %all_gather.9 = f32[32,4096]{1,0:T(8,128)S(1)} all-gather(f32[32,1024]{1,0:T(8,128)S(1)} %dynamic-slice_divide_fusion.2), channel_id=1, replica_groups=mesh['groups'=2,'row'=4,'col'=2,'rep'=2] {'row'}, dimensions={1}, use_global_device_ids=true | all-gather | bytes 655360 | tf_op jit(solution)/shard_map/all_gather | solution.py:26
  211.1 66.5 %fusion.7 = f32[32,4096]{1,0:T(8,128)} fusion(f32[32,4096]{1,0:T(8,128)S(1)} %all_gather.9, f32[4096,4096]{1,0:T(8,128)} %param.3), kind=kOutput, calls=%fused_computation.17 | convolution fusion | flops 6442450944 | bytes 68157440 | tf_op jit(solution)/shard_map/dot_general | solution.py:18
  277.6 0.0 all-reduce.14.cloned.1.call-start
  277.6 27.1 %all-reduce.12.cloned.1.call-done = f32[32,4096]{1,0:T(8,128)} async-done(((f32[32,4096]{1,0:T(8,128)}), f32[32,4096]{1,0:T(8,128)}) %all-reduce.12.cloned.1.call-update) | async-done | bytes 524304 | tf_op jit(solution)/shard_map/psum | solution.py:21
  304.8 0.2 reduce-scatter.6.cloned.1.call-start
  305.0 20.6 %all-reduce.14.cloned.1.call-done = f32[32,4096]{1,0:T(8,128)} async-done(((f32[32,4096]{1,0:T(8,128)}), f32[32,4096]{1,0:T(8,128)}) %all-reduce.14.cloned.1.call-update) | async-done | bytes 524304 | tf_op jit(solution)/shard_map/psum | solution.py:21
  325.6 44.8 %fusion = f32[32,4096]{1,0:T(8,128)} fusion(f32[4096,4096]{1,0:T(8,128)} %param.3, f32[32,4096]{1,0:T(8,128)S(1)} %copy-done, f32[32,4096]{1,0:T(8,128)} %all-reduce.14.cloned.1.call-done), kind=kOutput, calls=%fused_computation | convolution fusion | flops 6442582016 | bytes 68681728 | tf_op jit(solution)/shard_map/dot_general | solution.py:22
  370.4 0.0 all-reduce.16.cloned.1.call-start
  370.5 23.2 %reduce-scatter.6.cloned.1.call-done = f32[32,1024]{1,0:T(8,128)} async-done(((f32[32,4096]{1,0:T(8,128)}), f32[32,1024]{1,0:T(8,128)}) %reduce-scatter.6.cloned.1.call-update) | async-done | bytes 131088 | tf_op jit(solution)/shard_map/reduce_scatter | solution.py:25
  393.6 0.9 dynamic-slice_divide_fusion.1
  394.6 15.6 %all_gather.10 = f32[32,4096]{1,0:T(8,128)S(1)} all-gather(f32[32,1024]{1,0:T(8,128)S(1)} %dynamic-slice_divide_fusion.1), channel_id=1, replica_groups=mesh['groups'=2,'row'=4,'col'=2,'rep'=2] {'row'}, dimensions={1}, use_global_device_ids=true | all-gather | bytes 655360 | tf_op jit(solution)/shard_map/all_gather | solution.py:26
  410.2 66.5 %fusion.8 = f32[32,4096]{1,0:T(8,128)} fusion(f32[32,4096]{1,0:T(8,128)S(1)} %all_gather.10, f32[4096,4096]{1,0:T(8,128)} %param.3), kind=kOutput, calls=%fused_computation.18 | convolution fusion | flops 6442450944 | bytes 68157440 | tf_op jit(solution)/shard_map/dot_general | solution.py:18
  476.7 0.0 all-reduce.18.cloned.1.call-start
  476.7 27.2 %all-reduce.16.cloned.1.call-done = f32[32,4096]{1,0:T(8,128)} async-done(((f32[32,4096]{1,0:T(8,128)}), f32[32,4096]{1,0:T(8,128)}) %all-reduce.16.cloned.1.call-update) | async-done | bytes 524304 | tf_op jit(solution)/shard_map/psum | solution.py:21
  504.0 0.3 reduce-scatter.8.cloned.1.call-start
  504.3 20.7 %all-reduce.18.cloned.1.call-done = f32[32,4096]{1,0:T(8,128)} async-done(((f32[32,4096]{1,0:T(8,128)}), f32[32,4096]{1,0:T(8,128)}) %all-reduce.18.cloned.1.call-update) | async-done | bytes 524304 | tf_op jit(solution)/shard_map/psum | solution.py:21
  525.0 1.1 div.31
  526.1 45.0 %fusion.9 = f32[32,4096]{1,0:T(8,128)} fusion(f32[32,4096]{1,0:T(8,128)S(1)} %div.31, f32[4096,4096]{1,0:T(8,128)} %param.3), kind=kOutput, calls=%fused_computation.19 | convolution fusion | flops 6442450944 | bytes 68157440 | tf_op jit(solution)/shard_map/dot_general | solution.py:22
  571.1 23.2 %reduce-scatter.8.cloned.1.call-done = f32[32,1024]{1,0:T(8,128)} async-done(((f32[32,4096]{1,0:T(8,128)}), f32[32,1024]{1,0:T(8,128)}) %reduce-scatter.8.cloned.1.call-update) | async-done | bytes 131088 | tf_op jit(solution)/shard_map/reduce_scatter | solution.py:25
  594.3 1.1 abs_reduce_fusion.2
  595.4 15.5 %all_gather.11 = f32[32,4096]{1,0:T(8,128)S(1)} all-gather(f32[32,1024]{1,0:T(8,128)S(1)} %get-tuple-element.9), channel_id=1, replica_groups=mesh['groups'=2,'row'=4,'col'=2,'rep'=2] {'row'}, dimensions={1}, use_global_device_ids=true | all-gather | bytes 655360 | tf_op jit(solution)/shard_map/all_gather | solution.py:26
  610.9 29.5 %all-reduce = (f32[1,32]{1,0:T(1,128)S(1)}, f32[1,32]{1,0:T(1,128)S(1)}, f32[1,32]{1,0:T(1,128)S(1)}) all-reduce(f32[1,32]{1,0:T(1,128)S(1)} %get-tuple-element.10, f32[1,32]{1,0:T(1,128)S(1)} %get-tuple-element.11, f32[1,32]{1,0:T(1,128)S(1)} %multiply_bitcast_fusion.2), channel_id=1, replica_groups=mesh['groups'=2,'row'=4,'col'=2,'rep'=2] {'row','col','rep'}, use_global_device_ids=true, to_apply=%region_14.0 | all-reduce | flops 96 | bytes 768 | tf_op jit(solution)/shard_map/psum | solution.py:28
  640.4 0.6 pad_maximum_fusion
  641.0 0.8 copy.13
  (23 shorter events, 0.3 us)
Async XLA Ops:
  7.2 119.0 %copy-start = (f32[32,4096]{1,0:T(8,128)S(1)}, f32[32,4096]{1,0:T(8,128)}, u32[]{:S(2)}) copy-start(f32[32,4096]{1,0:T(8,128)} %param.4) | copy-start | bytes 1572868
  7.2 98.1 %all-reduce.8.cloned.1.call-start = ((), (), s32[]{:S(2)}) async-start(), calls=%async_computation.3 | async-start | bytes 1048576 | tf_op jit(solution)/shard_map/psum | solution.py:21
  73.7 120.6 %copy-start.4 = (f32[32,4096]{1,0:T(8,128)S(1)}, f32[32,4096]{1,0:T(8,128)}, u32[]{:S(2)}) copy-start(f32[32,4096]{1,0:T(8,128)} %param.5) | copy-start | bytes 1572868
  73.7 52.5 %all-reduce.10.cloned.1.call-start = ((), (), s32[]{:S(2)}) async-start(), calls=%async_computation.4 | async-start | bytes 1048576 | tf_op jit(solution)/shard_map/psum | solution.py:21
  105.3 89.0 %reduce-scatter.4.cloned.1.call-start = ((), (), s32[]{:S(2)}) async-start(), calls=%async_computation.5 | async-start | bytes 655360 | tf_op jit(solution)/shard_map/reduce_scatter | solution.py:25
  171.1 133.7 %all-reduce.12.cloned.1.call-start = ((), (), s32[]{:S(2)}) async-start(), calls=%async_computation.6 | async-start | bytes 1048576 | tf_op jit(solution)/shard_map/psum | solution.py:21
  277.6 48.0 %all-reduce.14.cloned.1.call-start = ((), (), s32[]{:S(2)}) async-start(), calls=%async_computation.7 | async-start | bytes 1048576 | tf_op jit(solution)/shard_map/psum | solution.py:21
  304.8 88.9 %reduce-scatter.6.cloned.1.call-start = ((), (), s32[]{:S(2)}) async-start(), calls=%async_computation.8 | async-start | bytes 655360 | tf_op jit(solution)/shard_map/reduce_scatter | solution.py:25
  370.4 133.5 %all-reduce.16.cloned.1.call-start = ((), (), s32[]{:S(2)}) async-start(), calls=%async_computation.9 | async-start | bytes 1048576 | tf_op jit(solution)/shard_map/psum | solution.py:21
  476.7 117.7 %copy-start.2 = (f32[32,1024]{1,0:T(8,128)S(1)}, f32[32,1024]{1,0:T(8,128)}, u32[]{:S(2)}) copy-start(f32[32,1024]{1,0:T(8,128)} %reduce-scatter.4.cloned.1.call-done) | copy-start | bytes 393220
  476.7 117.7 %copy-start.3 = (f32[32,1024]{1,0:T(8,128)S(1)}, f32[32,1024]{1,0:T(8,128)}, u32[]{:S(2)}) copy-start(f32[32,1024]{1,0:T(8,128)} %reduce-scatter.6.cloned.1.call-done) | copy-start | bytes 393220
  476.7 48.3 %all-reduce.18.cloned.1.call-start = ((), (), s32[]{:S(2)}) async-start(), calls=%async_computation.10 | async-start | bytes 1048576 | tf_op jit(solution)/shard_map/psum | solution.py:21
  504.0 90.3 %reduce-scatter.8.cloned.1.call-start = ((), (), s32[]{:S(2)}) async-start(), calls=%async_computation.11 | async-start | bytes 655360 | tf_op jit(solution)/shard_map/reduce_scatter | solution.py:25
  526.1 115.7 %copy-start.1 = (f32[32,4096]{1,0:T(8,128)}, f32[32,4096]{1,0:T(8,128)S(1)}, u32[]{:S(2)}) copy-start(f32[32,4096]{1,0:T(8,128)S(1)} %div.31) | copy-start | bytes 1572868
Sparse Core Ops, SparseCore 0:
  73.8 31.3 all-reduce.7
  107.6 18.5 all-reduce.9
  171.2 23.0 reduce-scatter.3
  277.7 26.9 all-reduce.11
  306.9 18.5 all-reduce.13
  370.6 23.0 reduce-scatter.5
  476.8 27.1 all-reduce.15
  506.3 18.5 all-reduce.17
  571.3 23.0 reduce-scatter.7
